TPU v7x, 32 devices: a whole 2x2x4 slice. The times are simulated.
32 devices in a mesh: ctx: 8 (over z, y), fsdp: 4 (over x, core).
Axes of the slice: x: 2, y: 2, z: 4, core: 2. Of those that a mesh axis runs over, the one named last changes fastest.
Arguments:
- tokens: bfloat16 [8192, 1024], P(('fsdp', 'ctx')), may hold values from -6 to 6
- cotangent: bfloat16 [8192, 1024], P(('fsdp', 'ctx')), may hold values from -6 to 6
- gain_attn: bfloat16 [1024], P('fsdp'), may hold values from 0.5 to 1.5
- w_qkv: bfloat16 [1024, 3072], P('fsdp'), may hold values from -0.25 to 0.25
- w_out: bfloat16 [1024, 1024], P('fsdp'), may hold values from -0.75 to 0.75
- gain_ffn: bfloat16 [1024], P('fsdp'), may hold values from 0.5 to 1.5
- w_gate_up: bfloat16 [1024, 5632], P('fsdp'), may hold values from -0.1875 to 0.1875
- w_down: bfloat16 [2816, 1024], P('fsdp'), may hold values from -0.109375 to 0.109375
- lengths: int32 [4, 4], P('fsdp'), may hold values from 1 to 1024, 2048 in all within a row
- block_order: int32 [4, 32], P('fsdp'), may hold values from 0 to 31, each once within a row
Outputs:
- output: bfloat16 [8192, 1024], P(('fsdp', 'ctx'))
- grad_tokens: bfloat16 [8192, 1024], P(('fsdp', 'ctx'))
- grad_gain_attn: float32 [1024], P('fsdp')
- grad_w_qkv: float32 [1024, 3072], P('fsdp')
- grad_w_out: float32 [1024, 1024], P('fsdp')
- grad_gain_ffn: float32 [1024], P('fsdp')
- grad_w_gate_up: float32 [1024, 5632], P('fsdp')
- grad_w_down: float32 [2816, 1024], P('fsdp')
Inputs may be any that keep to these rules, and one draw needn't show every extreme that they name: Each row gives the lengths of the 4 sequences that fill one group's 2048 tokens, in sequence order; the longest is exactly 1024. `block_order`: each row is a permutation of the 32 blocks of one group.
All inputs are finite; a program needn't handle non-finite values.
Results may differ from a plain program's by a relative error of at most 0.024.
Values may be sent and summed in bfloat16 or wider, within the bound.
No kernel may reach another device: no remote copies, remote signals or barrier semaphores. Data moves between devices by JAX's collectives and lax.ppermute only.
A program may use at most 256 MiB of HBM per device.

v0:
```python
import math
import jax
import jax.numpy as jnp
from jax import lax
from jax.sharding import PartitionSpec as P

HEADS = 16
EPS = 1e-05
MASKED = -1e30


def contract_rows(left, right):
    return lax.dot_general(
        left, right, (((0,), (0,)), ((), ())), preferred_element_type=jnp.float32
    )


def against_rows(left, right):
    return lax.dot_general(
        left, right, (((1,), (1,)), ((), ())), preferred_element_type=jnp.float32
    )


def rms_forward(rows):
    inverse = lax.rsqrt(jnp.mean(rows * rows, axis=1, keepdims=True) + EPS)
    return (rows * inverse, inverse)


def rms_backward(normed, inverse, gain, grad_out):
    scaled = grad_out * gain
    inner = jnp.mean(scaled * normed, axis=1, keepdims=True)
    return (inverse * (scaled - normed * inner), jnp.sum(grad_out * normed, axis=0))


def visible(pos_query, seg_query, pos_keys, seg_keys):
    return (seg_query[:, None] == seg_keys[None, :]) & (pos_keys[None, :] <= pos_query[:, None])


def key_block(kv_all, pos_all, seg_all, start, block_rows, heads, depth):
    width = heads * depth
    kv_block = lax.dynamic_slice_in_dim(kv_all, start, block_rows, 0)
    key_heads = kv_block[:, :width].reshape(block_rows, heads, depth)
    value_heads = kv_block[:, width:].reshape(block_rows, heads, depth)
    pos_block = lax.dynamic_slice_in_dim(pos_all, start, block_rows, 0)
    seg_block = lax.dynamic_slice_in_dim(seg_all, start, block_rows, 0)
    return (key_heads, value_heads, pos_block, seg_block)


def attend_forward(query_heads, kv_all, pos_query, seg_query, pos_all, seg_all, scale):
    rows, heads, depth = query_heads.shape
    total_keys = kv_all.shape[0]
    block_rows = min(512, total_keys)

    def one_step(carry, number):
        run_max, run_sum, accum = carry
        key_heads, value_heads, pos_block, seg_block = key_block(
            kv_all, pos_all, seg_all, number * block_rows, block_rows, heads, depth
        )
        allowed = visible(pos_query, seg_query, pos_block, seg_block)[:, None, :]
        scores = (
            jnp.einsum("qhd,khd->qhk", query_heads, key_heads, preferred_element_type=jnp.float32)
            * scale
        )
        scores = jnp.where(allowed, scores, MASKED)
        new_max = jnp.maximum(run_max, jnp.max(scores, axis=2))
        expo = jnp.where(allowed, jnp.exp(scores - new_max[:, :, None]), 0.0)
        factor = jnp.exp(run_max - new_max)
        run_sum = run_sum * factor + jnp.sum(expo, axis=2)
        accum = accum * factor[:, :, None] + jnp.einsum(
            "qhk,khd->qhd",
            expo.astype(jnp.bfloat16),
            value_heads,
            preferred_element_type=jnp.float32,
        )
        return ((new_max, run_sum, accum), None)

    start_state = (
        jnp.full((rows, heads), MASKED, jnp.float32),
        jnp.zeros((rows, heads), jnp.float32),
        jnp.zeros((rows, heads, depth), jnp.float32),
    )
    final_state, unused = lax.scan(
        one_step, start_state, jnp.arange(total_keys // block_rows, dtype=jnp.int32)
    )
    run_max, run_sum, accum = final_state
    return (accum / run_sum[:, :, None], run_max + jnp.log(run_sum))


def attend_backward(
    query_heads, kv_all, grad_heads, delta, log_total, pos_query, seg_query, pos_all, seg_all, scale
):
    rows, heads, depth = query_heads.shape
    width = heads * depth
    total_keys = kv_all.shape[0]
    block_rows = min(512, total_keys)

    def one_step(grad_query, number):
        key_heads, value_heads, pos_block, seg_block = key_block(
            kv_all, pos_all, seg_all, number * block_rows, block_rows, heads, depth
        )
        allowed = visible(pos_query, seg_query, pos_block, seg_block)[:, None, :]
        scores = (
            jnp.einsum("qhd,khd->qhk", query_heads, key_heads, preferred_element_type=jnp.float32)
            * scale
        )
        probs = jnp.where(allowed, jnp.exp(scores - log_total[:, :, None]), 0.0)
        dprob = jnp.einsum(
            "qhd,khd->qhk", grad_heads, value_heads, preferred_element_type=jnp.float32
        )
        grad_scores = (probs * (dprob - delta[:, :, None])).astype(jnp.bfloat16)
        grad_query = grad_query + jnp.einsum(
            "qhk,khd->qhd", grad_scores, key_heads, preferred_element_type=jnp.float32
        )
        grad_keys = (
            jnp.einsum("qhk,qhd->khd", grad_scores, query_heads, preferred_element_type=jnp.float32)
            * scale
        )
        grad_values = jnp.einsum(
            "qhk,qhd->khd",
            probs.astype(jnp.bfloat16),
            grad_heads,
            preferred_element_type=jnp.float32,
        )
        return (
            grad_query,
            jnp.concatenate(
                [grad_keys.reshape(block_rows, width), grad_values.reshape(block_rows, width)],
                axis=1,
            ),
        )

    grad_query, grad_pairs = lax.scan(
        one_step,
        jnp.zeros((rows, heads, depth), jnp.float32),
        jnp.arange(total_keys // block_rows, dtype=jnp.int32),
    )
    return (grad_query * scale, grad_pairs.reshape(total_keys, 2 * width))


def body(
    tokens, cotangent, gain_attn, w_qkv, w_out, gain_ffn, w_gate_up, w_down, lengths, block_order
):
    rows, width = tokens.shape
    heads = HEADS
    depth = width // heads
    scale = depth ** (-0.5)
    ctx_count = lax.axis_size("ctx")
    fsdp_count = lax.axis_size("fsdp")
    group_rows = rows * ctx_count
    factor = 1.0 / math.sqrt(rows * ctx_count * fsdp_count)
    gathered = (
        lax.all_gather(gain_attn, "fsdp", axis=0, tiled=True),
        lax.all_gather(w_qkv, "fsdp", axis=0, tiled=True),
        lax.all_gather(w_out, "fsdp", axis=0, tiled=True),
        lax.all_gather(gain_ffn, "fsdp", axis=0, tiled=True),
        lax.all_gather(w_gate_up, "fsdp", axis=0, tiled=True),
        lax.all_gather(w_down, "fsdp", axis=0, tiled=True),
    )
    gain_one, weight_qkv, weight_out, gain_two, weight_gu, weight_down = gathered
    gain_one = gain_one.astype(jnp.float32)
    gain_two = gain_two.astype(jnp.float32)
    hidden_width = weight_down.shape[0]
    block_size = group_rows // block_order.shape[1]
    pos_all = (
        block_order[0][:, None] * block_size + jnp.arange(block_size, dtype=jnp.int32)[None, :]
    ).reshape(group_rows)
    ends = jnp.cumsum(lengths[0])
    seg_all = jnp.sum((pos_all[:, None] >= ends[None, :]).astype(jnp.int32), axis=1)
    offset = lax.axis_index("ctx") * rows
    pos_query = lax.dynamic_slice_in_dim(pos_all, offset, rows, 0)
    seg_query = lax.dynamic_slice_in_dim(seg_all, offset, rows, 0)
    inputs = tokens.astype(jnp.float32)
    normed_one, inverse_one = rms_forward(inputs)
    attn_in = (normed_one * gain_one).astype(jnp.bfloat16)
    qkv = jnp.dot(attn_in, weight_qkv, preferred_element_type=jnp.float32).astype(jnp.bfloat16)
    query_flat = qkv[:, :width]
    query_heads = query_flat.reshape(rows, heads, depth)
    key_value = qkv[:, width:]
    kv_all = lax.all_gather(key_value, "ctx", axis=0, tiled=True)
    out_heads, log_total = attend_forward(
        query_heads, kv_all, pos_query, seg_query, pos_all, seg_all, scale
    )
    attn_low = out_heads.reshape(rows, width).astype(jnp.bfloat16)
    resid = inputs + jnp.dot(attn_low, weight_out, preferred_element_type=jnp.float32)
    normed_two, inverse_two = rms_forward(resid)
    ffn_in = (normed_two * gain_two).astype(jnp.bfloat16)
    gate_up = jnp.dot(ffn_in, weight_gu, preferred_element_type=jnp.float32)
    gate = gate_up[:, :hidden_width]
    upward = gate_up[:, hidden_width:]
    sigma = jax.nn.sigmoid(gate)
    active = gate * sigma
    hidden = (active * upward).astype(jnp.bfloat16)
    output = (resid + jnp.dot(hidden, weight_down, preferred_element_type=jnp.float32)).astype(
        jnp.bfloat16
    )
    grad_hidden = against_rows(cotangent, weight_down)
    grad_gate = grad_hidden * upward * (sigma + gate * sigma * (1.0 - sigma))
    grad_up = grad_hidden * active
    grad_gu = jnp.concatenate([grad_gate, grad_up], axis=1).astype(jnp.bfloat16)
    grad_ffn_in = against_rows(grad_gu, weight_gu)
    grad_norm_two, grad_gain_two = rms_backward(normed_two, inverse_two, gain_two, grad_ffn_in)
    grad_resid = cotangent.astype(jnp.float32) + grad_norm_two
    grad_branch = grad_resid.astype(jnp.bfloat16)
    grad_attn = against_rows(grad_branch, weight_out).astype(jnp.bfloat16)
    grad_heads = grad_attn.reshape(rows, heads, depth)
    delta = jnp.sum(grad_heads.astype(jnp.float32) * out_heads, axis=2)
    kv_back = lax.all_gather(key_value, "ctx", axis=0, tiled=True)
    grad_query, grad_pair_terms = attend_backward(
        query_heads,
        kv_back,
        grad_heads,
        delta,
        log_total,
        pos_query,
        seg_query,
        pos_all,
        seg_all,
        scale,
    )
    grad_pairs = lax.psum_scatter(
        grad_pair_terms.astype(jnp.bfloat16), "ctx", scatter_dimension=0, tiled=True
    )
    grad_qkv = jnp.concatenate(
        [grad_query.reshape(rows, width).astype(jnp.bfloat16), grad_pairs], axis=1
    )
    grad_attn_in = against_rows(grad_qkv, weight_qkv)
    grad_norm_one, grad_gain_one = rms_backward(normed_one, inverse_one, gain_one, grad_attn_in)
    grad_tokens = (grad_resid + grad_norm_one).astype(jnp.bfloat16)
    terms = (
        grad_gain_one,
        contract_rows(attn_in, grad_qkv),
        contract_rows(attn_low, grad_branch),
        grad_gain_two,
        contract_rows(ffn_in, grad_gu),
        contract_rows(hidden, cotangent),
    )
    partial_shards = (
        lax.psum_scatter(
            terms[0].astype(jnp.bfloat16), "fsdp", scatter_dimension=0, tiled=True
        ).astype(jnp.float32),
        lax.psum_scatter(
            terms[1].astype(jnp.bfloat16), "fsdp", scatter_dimension=0, tiled=True
        ).astype(jnp.float32),
        lax.psum_scatter(
            terms[2].astype(jnp.bfloat16), "fsdp", scatter_dimension=0, tiled=True
        ).astype(jnp.float32),
        lax.psum_scatter(
            terms[3].astype(jnp.bfloat16), "fsdp", scatter_dimension=0, tiled=True
        ).astype(jnp.float32),
        lax.psum_scatter(
            terms[4].astype(jnp.bfloat16), "fsdp", scatter_dimension=0, tiled=True
        ).astype(jnp.float32),
        lax.psum_scatter(
            terms[5].astype(jnp.bfloat16), "fsdp", scatter_dimension=0, tiled=True
        ).astype(jnp.float32),
    )
    shards = (
        lax.psum(partial_shards[0].astype(jnp.bfloat16), "ctx").astype(jnp.float32),
        lax.psum(partial_shards[1].astype(jnp.bfloat16), "ctx").astype(jnp.float32),
        lax.psum(partial_shards[2].astype(jnp.bfloat16), "ctx").astype(jnp.float32),
        lax.psum(partial_shards[3].astype(jnp.bfloat16), "ctx").astype(jnp.float32),
        lax.psum(partial_shards[4].astype(jnp.bfloat16), "ctx").astype(jnp.float32),
        lax.psum(partial_shards[5].astype(jnp.bfloat16), "ctx").astype(jnp.float32),
    )
    return (
        output,
        grad_tokens,
        shards[0] * factor,
        shards[1] * factor,
        shards[2] * factor,
        shards[3] * factor,
        shards[4] * factor,
        shards[5] * factor,
    )


def solution(mesh):
    in_specs = (
        P(("fsdp", "ctx"), None),
        P(("fsdp", "ctx"), None),
        P("fsdp"),
        P("fsdp", None),
        P("fsdp", None),
        P("fsdp"),
        P("fsdp", None),
        P("fsdp", None),
        P("fsdp", None),
        P("fsdp", None),
    )
    out_specs = (
        P(("fsdp", "ctx"), None),
        P(("fsdp", "ctx"), None),
        P("fsdp"),
        P("fsdp", None),
        P("fsdp", None),
        P("fsdp"),
        P("fsdp", None),
        P("fsdp", None),
    )
    return jax.shard_map(body, mesh=mesh, in_specs=in_specs, out_specs=out_specs, check_vma=False)
```

profile of v0, /device:TPU:0, one launch (start us, length us, event | category | flops | bytes accessed | tf_op | source)
XLA Modules:
  0.0 1096.1 jit_solution(1279736065175315214)
XLA Ops:
  8.6 6.0 all-gather
  15.8 42.8 %all-gather.8.cloned.1.call-done = bf16[1024,3072]{1,0:T(8,128)(2,1)} async-done(((bf16[256,3072]{1,0:T(8,128)(2,1)}), bf16[1024,3072]{1,0:T(8,128)(2,1)}) %all-gather.8.cloned.1.call-update) | async-done | bytes 6291472 | tf_op jit(solution)/shard_map/all_gather | solution.py:153
  58.7 4.8 convolution_convert_fusion.3
  67.3 5.2 all-gather.1
  72.8 117.0 %all-gather.10.cloned.1.call-done = bf16[2048,2048]{1,0:T(8,128)(2,1)} async-done(((bf16[256,2048]{1,0:T(8,128)(2,1)}), bf16[2048,2048]{1,0:T(8,128)(2,1)}) %all-gather.10.cloned.1.call-update) | async-done | bytes 8388624 | tf_op jit(solution)/shard_map/all_gather | solution.py:179
  189.8 12.4 %copy.64 = bf16[2048,2048]{0,1:T(8,128)(2,1)} copy(bf16[2048,2048]{1,0:T(8,128)(2,1)} %all-gather.10.cloned.1.call-done) | data formatting | bytes 16777216
  202.1 73.7 %while.28 = (s32[]{:T(128)}, f32[256,16]{0,1:T(8,128)S(1)}, f32[256,16]{0,1:T(8,128)S(1)}, f32[256,16,64]{0,2,1:T(8,128)}, s32[256]{0:T(256)S(1)}, /*index=5*/s3...) while((s32[]{:T(128)}, f32[256,16]{0,1:T(8,128)S(1)}, ...), condition=%wide.region_6.7_spmd.clone, body=%wide.region_3.6_spmd.clone.sunk | while | flops 565334016 | bytes 68434200 | solution.py:82
  205.4 4.8 fusion.113
  222.9 6.1 fusion.113
  279.8 9.9 all-gather.14.cloned.1.call-done
  289.7 9.4 fusion.54
  299.1 35.4 %all-gather.16.cloned.1.call-done = bf16[2816,1024]{1,0:T(8,128)(2,1)} async-done(((bf16[704,1024]{1,0:T(8,128)(2,1)}), bf16[2816,1024]{1,0:T(8,128)(2,1)}) %all-gather.16.cloned.1.call-update) | async-done | bytes 5767184 | tf_op jit(solution)/shard_map/all_gather | solution.py:157
  334.6 8.8 multiply_convert_fusion.1
  343.4 7.5 multiply_reduce_fusion
  356.2 102.9 %while.29 = (s32[]{:T(128)}, f32[256,16,64]{0,2,1:T(8,128)}, bf16[4,512,2048]{2,1,0:T(8,128)(2,1)}, s32[4]{0:T(128)S(1)}, bf16[2048,2048]{0,1:T(8,128)(2,1)}, /*...) while((s32[]{:T(128)}, f32[256,16,64]{0,2,1:T(8,128)}, ...), condition=%wide.region_11.12_spmd.clone, body=%wide.region_10.11_spmd.clone.sunk | while | flops 1369309184 | bytes 118946184 | solution.py:132
  369.2 5.2 fusion.131
  395.0 5.2 fusion.131
  420.8 5.2 fusion.131
  446.6 5.2 fusion.131
  462.5 5.6 convolution_convert_fusion.1
  469.4 7.9 convolution_convert_fusion
  480.8 127.4 %reduce-scatter.6.cloned.1.call-done = bf16[256,2048]{1,0:T(8,128)(2,1)} async-done(((bf16[2048,2048]{1,0:T(8,128)(2,1)}), bf16[256,2048]{1,0:T(8,128)(2,1)}) %reduce-scatter.6.cloned.1.call-update) | async-done | bytes 1048592 | tf_op jit(solution)/shard_map/reduce_scatter | solution.py:220
  608.2 5.8 convolution_convert_fusion.2
  614.1 27.8 %reduce-scatter.10.cloned.1.call-done = bf16[256,1024]{1,0:T(8,128)(2,1)} async-done(((bf16[1024,1024]{1,0:T(8,128)(2,1)}), bf16[256,1024]{1,0:T(8,128)(2,1)}) %reduce-scatter.10.cloned.1.call-update) | async-done | bytes 524304 | tf_op jit(solution)/shard_map/reduce_scatter | solution.py:244
  641.9 58.0 %reduce-scatter.14.cloned.1.call-done = bf16[704,1024]{1,0:T(8,128)(2,1)} async-done(((bf16[2816,1024]{1,0:T(8,128)(2,1)}), bf16[704,1024]{1,0:T(8,128)(2,1)}) %reduce-scatter.14.cloned.1.call-update) | async-done | bytes 1441808 | tf_op jit(solution)/shard_map/reduce_scatter | solution.py:253
  699.9 95.0 %reduce-scatter.12.cloned.1.call-done = bf16[256,5632]{1,0:T(8,128)(2,1)} async-done(((bf16[1024,5632]{1,0:T(8,128)(2,1)}), bf16[256,5632]{1,0:T(8,128)(2,1)}) %reduce-scatter.12.cloned.1.call-update) | async-done | bytes 2883600 | tf_op jit(solution)/shard_map/reduce_scatter | solution.py:250
  794.9 61.0 %reduce-scatter.8.cloned.1.call-done = bf16[256,3072]{1,0:T(8,128)(2,1)} async-done(((bf16[1024,3072]{1,0:T(8,128)(2,1)}), bf16[256,3072]{1,0:T(8,128)(2,1)}) %reduce-scatter.8.cloned.1.call-update) | async-done | bytes 1572880 | tf_op jit(solution)/shard_map/reduce_scatter | solution.py:241
  857.1 5.6 fusion.35
  862.8 4.8 fusion.42
  867.6 6.1 all-reduce.4
  873.8 22.6 %all-reduce.2 = (bf16[256]{0:T(256)(128)(2,1)S(1)}, bf16[256]{0:T(256)(128)(2,1)S(1)}) all-reduce(bf16[256]{0:T(256)(128)(2,1)S(1)} %dynamic-slice.1, bf16[256]{0:T(256)(128)(2,1)S(1)} %dynamic-slice.3), channel_id=1, replica_groups=mesh['ctx'=8,'fsdp'=4] {'ctx'}, use_global_device_ids=true, to_apply=%region_16.17 | all-reduce | flops 512 | bytes 2048 | tf_op jit(solution)/shard_map/psum | solution.py:258
  898.1 181.6 %all-reduce.7.cloned.1.call-done = (bf16[256,3072]{1,0:T(8,128)(2,1)}, bf16[256,1024]{1,0:T(8,128)(2,1)}, bf16[256,5632]{1,0:T(8,128)(2,1)}, bf16[704,1024]{1,0:T(8,128)(2,1)}) async-done(((bf16[256,3072]{1,0:T(8,128)(2,1)}, bf16[256,1024]{1,0:T(8,128)(2,1)}, bf16[256,5632]{1,0:T(8,128)(2,1)}, bf16[704,1024]{1,0:T(8,128)(2,1)}), (bf16[256,3072]{1,0:T(8,128)(2,1)}, bf16[256,1024]{1,0:T(8,128)(2,1)}, ...) | async-done | bytes 6422544 | tf_op jit(solution)/shard_map/psum | solution.py:259
  (250 shorter events, 175.2 us)
Async XLA Ops:
  7.2 51.5 %all-gather.8.cloned.1.call-start = ((), (), s32[]{:S(2)}) async-start(), calls=%async_computation.5 | async-start | bytes 7864320 | tf_op jit(solution)/shard_map/all_gather | solution.py:153
  7.9 181.9 %all-gather.10.cloned.1.call-start = ((), (), s32[]{:S(2)}) async-start(), calls=%async_computation.6 | async-start | bytes 9437184 | tf_op jit(solution)/shard_map/all_gather | solution.py:179
  14.6 48.9 %copy-start.23 = (f32[4,1,256]{2,1,0:T(1,128)}, f32[4,1,256]{2,1,0:T(1,128)S(1)}, u32[]{:S(2)}) copy-start(f32[4,1,256]{2,1,0:T(1,128)S(1)} %convert_element_type.150) | copy-start | bytes 12292
  15.8 47.7 %copy-start.25 = (f32[256]{0:T(256)}, f32[256]{0:T(256)S(1)}, u32[]{:S(2)}) copy-start(f32[256]{0:T(256)S(1)} %add_rsqrt_fusion.1) | copy-start | bytes 3076
  64.7 212.5 %all-gather.12.cloned.1.call-start = ((), (), s32[]{:S(2)}) async-start(), calls=%async_computation.7 | async-start | bytes 2621440 | tf_op jit(solution)/shard_map/all_gather | solution.py:154
  65.4 224.3 %all-gather.14.cloned.1.call-start = ((), (), s32[]{:S(2)}) async-start(), calls=%async_computation.8 | async-start | bytes 14417920 | tf_op jit(solution)/shard_map/all_gather | solution.py:156
  66.0 268.6 %all-gather.16.cloned.1.call-start = ((), (), s32[]{:S(2)}) async-start(), calls=%async_computation.9 | async-start | bytes 7208960 | tf_op jit(solution)/shard_map/all_gather | solution.py:157
  66.6 541.7 %reduce-scatter.6.cloned.1.call-start = ((), (), s32[]{:S(2)}) async-start(), calls=%async_computation.10 | async-start | bytes 9437184 | tf_op jit(solution)/shard_map/reduce_scatter | solution.py:220
  202.1 75.1 %copy-start.8 = (bf16[256,1024]{1,0:T(8,128)(2,1)S(1)}, bf16[256,1024]{1,0:T(8,128)(2,1)}, u32[]{:S(2)}) copy-start(bf16[256,1024]{1,0:T(8,128)(2,1)} %param.14) | copy-start | bytes 1572868
  210.2 5.9 copy-start
  229.0 5.8 copy-start
  247.2 6.0 copy-start
  265.6 5.9 copy-start
  277.2 22.0 %copy-start.9 = (bf16[256,16,64]{0,2,1:T(8,128)(2,1)}, bf16[256,16,64]{0,2,1:T(8,128)(2,1)S(1)}, u32[]{:S(2)}) copy-start(bf16[256,16,64]{0,2,1:T(8,128)(2,1)S(1)} %fusion.45) | copy-start | bytes 1572868
  279.8 71.2 %copy-start.3 = (f32[256,1024]{1,0:T(8,128)}, f32[256,1024]{1,0:T(8,128)S(1)}, u32[]{:S(2)}) copy-start(f32[256,1024]{1,0:T(8,128)S(1)} %get-tuple-element.410) | copy-start | bytes 3145732
  289.7 44.9 %copy-start.15 = (bf16[256,1024]{1,0:T(8,128)(2,1)S(1)}, bf16[256,1024]{1,0:T(8,128)(2,1)}, u32[]{:S(2)}) copy-start(bf16[256,1024]{1,0:T(8,128)(2,1)} %param.15) | copy-start | bytes 1572868
  343.4 7.6 copy-start.19
  343.4 7.6 copy-start.20
  343.4 7.6 copy-start.16
  343.4 7.9 copy-start.7
  369.2 5.2 copy-start.1
  395.0 5.2 copy-start.1
  420.8 5.2 copy-start.1
  459.1 182.8 %reduce-scatter.10.cloned.1.call-start = ((), (), s32[]{:S(2)}) async-start(), calls=%async_computation.12 | async-start | bytes 2621440 | tf_op jit(solution)/shard_map/reduce_scatter | solution.py:244
  462.5 237.5 %reduce-scatter.14.cloned.1.call-start = ((), (), s32[]{:S(2)}) async-start(), calls=%async_computation.14 | async-start | bytes 7208960 | tf_op jit(solution)/shard_map/reduce_scatter | solution.py:253
  468.2 326.7 %reduce-scatter.12.cloned.1.call-start = ((), (), s32[]{:S(2)}) async-start(), calls=%async_computation.13 | async-start | bytes 14417920 | tf_op jit(solution)/shard_map/reduce_scatter | solution.py:250
  477.3 130.9 %copy-start.24 = (f32[4,1,256]{2,1,0:T(1,128)S(1)}, f32[4,1,256]{2,1,0:T(1,128)}, u32[]{:S(2)}) copy-start(f32[4,1,256]{2,1,0:T(1,128)} %copy-done.23) | copy-start | bytes 12292
  477.3 130.9 %copy-start.26 = (f32[256]{0:T(256)S(1)}, f32[256]{0:T(256)}, u32[]{:S(2)}) copy-start(f32[256]{0:T(256)} %copy-done.25) | copy-start | bytes 3076
  477.3 378.5 %reduce-scatter.8.cloned.1.call-start = ((), (), s32[]{:S(2)}) async-start(), calls=%async_computation.11 | async-start | bytes 7864320 | tf_op jit(solution)/shard_map/reduce_scatter | solution.py:241
  614.1 241.8 %copy-start.30 = (u32[32]{0:T(128)S(1)}, u32[32]{0:T(128)}, u32[]{:S(2)}) copy-start(u32[32]{0:T(128)} %constant.83) | copy-start | bytes 388
  614.1 465.5 %all-reduce.7.cloned.1.call-start = ((), (), s32[]{:S(2)}) async-start(), calls=%async_computation.15 | async-start | bytes 12845056 | tf_op jit(solution)/shard_map/psum | solution.py:259
  857.1 5.6 copy-start.21
  (25 other events, 85.2 us)
Sparse Core Ops, SparseCore 0:
  9.6 49.0 all-gather.7
  64.8 124.9 all-gather.9
  191.3 20.7 all-gather.11
  213.5 76.1 all-gather.13
  291.1 43.3 all-gather.15
  459.2 148.9 reduce-scatter.5
  611.5 30.4 reduce-scatter.9
  645.0 54.8 reduce-scatter.13
  702.7 92.1 reduce-scatter.11
  797.5 58.3 reduce-scatter.7
  860.5 219.0 all-reduce.6
where the time goes:
time: 1100 us
  waiting for transfers between devices  758 us (69%)
  matrix products  169 us (15%)
  local copies, waits for them, and re-layouts  63.6 us (6%)
  other arithmetic  44.1 us (4%)
  blocking collectives  39.9 us (4%)
  between operations  14.9 us (1%)
    psum x1, waiting for transfers between devices, body(): lax.psum(partial_shards[1].astype(jnp.bfloat16), 'ctx').astype(jnp.float32)  182 us
    reduce_scatter x1, waiting for transfers between devices, body(): lax.psum_scatter(grad_pair_terms.astype(jnp.bfloat16), 'ctx', scatter_dim...  127 us
    all_gather x1, waiting for transfers between devices, body(): kv_all = lax.all_gather(key_value, 'ctx', axis=0, tiled=True)  117 us
    reduce_scatter x1, waiting for transfers between devices, body(): lax.psum_scatter(terms[4].astype(jnp.bfloat16), 'fsdp', scatter_dimension...  95 us
    reduce_scatter x1, waiting for transfers between devices, body(): lax.psum_scatter(terms[1].astype(jnp.bfloat16), 'fsdp', scatter_dimension...  61 us
    reduce_scatter x1, waiting for transfers between devices, body(): lax.psum_scatter(terms[5].astype(jnp.bfloat16), 'fsdp', scatter_dimension...  58 us
    all_gather x1, waiting for transfers between devices, body(): lax.all_gather(w_qkv, 'fsdp', axis=0, tiled=True)  42.8 us
    all_gather x1, waiting for transfers between devices, body(): lax.all_gather(w_down, 'fsdp', axis=0, tiled=True)  35.4 us
  transfers between devices with their start and end apart: 11, of which 10 were waited for; matrix products, arithmetic and copies ran while one was open for 12% of the time, Pallas kernels for 0%

commit v1 on v0

--- a/solution.py
+++ b/solution.py
@@ -256,7 +256,9 @@
     )
     shards = (
         lax.psum(partial_shards[0].astype(jnp.bfloat16), "ctx").astype(jnp.float32),
-        lax.psum(partial_shards[1].astype(jnp.bfloat16), "ctx").astype(jnp.float32),
+        jnp.sum(lax.all_gather(partial_shards[1].astype(jnp.bfloat16), "ctx"), axis=0).astype(
+            jnp.float32
+        ),
         lax.psum(partial_shards[2].astype(jnp.bfloat16), "ctx").astype(jnp.float32),
         lax.psum(partial_shards[3].astype(jnp.bfloat16), "ctx").astype(jnp.float32),
         lax.psum(partial_shards[4].astype(jnp.bfloat16), "ctx").astype(jnp.float32),

time: 1100 us -> 1230 us (1.12)
  waiting for transfers between devices: 758 us -> 882 us
    all_gather x0 -> x1, waiting for transfers between devices: none -> 169 us  [body(): lax.all_gather(partial_shards[1].astype(jnp.bfloat16), 'ctx')]
    psum x1, waiting for transfers between devices: 182 us -> 137 us  [body(): lax.psum(partial_shards[2].astype(jnp.bfloat16), 'ctx').astype(jnp.float32)]
  transfers between devices with their start and end apart: 11 -> 12, of which waited for: 10 -> 11; matrix products, arithmetic and copies ran while one was open for 12% -> 11% of each run, Pallas kernels for 0% -> 0%
where the time goes in v1:
time: 1230 us
  waiting for transfers between devices  882 us (72%)
  matrix products  170 us (14%)
  local copies, waits for them, and re-layouts  63.7 us (5%)
  other arithmetic  52.3 us (4%)
  blocking collectives  39.5 us (3%)
  between operations  15.4 us (1%)
    all_gather x1, waiting for transfers between devices, body(): lax.all_gather(partial_shards[1].astype(jnp.bfloat16), 'ctx')  169 us
    psum x1, waiting for transfers between devices, body(): lax.psum(partial_shards[2].astype(jnp.bfloat16), 'ctx').astype(jnp.float32)  137 us
    reduce_scatter x1, waiting for transfers between devices, body(): lax.psum_scatter(grad_pair_terms.astype(jnp.bfloat16), 'ctx', scatter_dim...  127 us
    all_gather x1, waiting for transfers between devices, body(): kv_all = lax.all_gather(key_value, 'ctx', axis=0, tiled=True)  117 us
    reduce_scatter x1, waiting for transfers between devices, body(): lax.psum_scatter(terms[4].astype(jnp.bfloat16), 'fsdp', scatter_dimension...  95 us
    reduce_scatter x1, waiting for transfers between devices, body(): lax.psum_scatter(terms[1].astype(jnp.bfloat16), 'fsdp', scatter_dimension...  60.9 us
    reduce_scatter x1, waiting for transfers between devices, body(): lax.psum_scatter(terms[5].astype(jnp.bfloat16), 'fsdp', scatter_dimension...  58 us
    all_gather x1, waiting for transfers between devices, body(): lax.all_gather(w_qkv, 'fsdp', axis=0, tiled=True)  42.8 us
  transfers between devices with their start and end apart: 12, of which 11 were waited for; matrix products, arithmetic and copies ran while one was open for 11% of the time, Pallas kernels for 0%

profile of v1, /device:TPU:0, one launch (start us, length us, event | category | flops | bytes accessed | tf_op | source)
XLA Modules:
  0.0 1228.8 jit_solution(15004018017837106554)
XLA Ops:
  8.6 6.0 all-gather.1
  15.8 42.8 %all-gather.10.cloned.1.call-done = bf16[1024,3072]{1,0:T(8,128)(2,1)} async-done(((bf16[256,3072]{1,0:T(8,128)(2,1)}), bf16[1024,3072]{1,0:T(8,128)(2,1)}) %all-gather.10.cloned.1.call-update) | async-done | bytes 6291472 | tf_op jit(solution)/shard_map/all_gather | solution.py:153
  67.3 5.3 all-gather.2
  72.8 116.9 %all-gather.12.cloned.1.call-done = bf16[2048,2048]{1,0:T(8,128)(2,1)} async-done(((bf16[256,2048]{1,0:T(8,128)(2,1)}), bf16[2048,2048]{1,0:T(8,128)(2,1)}) %all-gather.12.cloned.1.call-update) | async-done | bytes 8388624 | tf_op jit(solution)/shard_map/all_gather | solution.py:179
  189.8 12.4 %copy.64 = bf16[2048,2048]{0,1:T(8,128)(2,1)} copy(bf16[2048,2048]{1,0:T(8,128)(2,1)} %all-gather.12.cloned.1.call-done) | data formatting | bytes 16777216
  202.1 73.7 %while.28 = (s32[]{:T(128)}, f32[256,16]{0,1:T(8,128)S(1)}, f32[256,16]{0,1:T(8,128)S(1)}, f32[256,16,64]{0,2,1:T(8,128)}, s32[256]{0:T(256)S(1)}, /*index=5*/s3...) while((s32[]{:T(128)}, f32[256,16]{0,1:T(8,128)S(1)}, ...), condition=%wide.region_6.7_spmd.clone, body=%wide.region_3.6_spmd.clone.sunk | while | flops 565334016 | bytes 68434200 | solution.py:82
  222.9 6.1 fusion.113
  279.8 9.9 all-gather.16.cloned.1.call-done
  289.7 9.4 fusion.54
  299.1 35.4 %all-gather.18.cloned.1.call-done = bf16[2816,1024]{1,0:T(8,128)(2,1)} async-done(((bf16[704,1024]{1,0:T(8,128)(2,1)}), bf16[2816,1024]{1,0:T(8,128)(2,1)}) %all-gather.18.cloned.1.call-update) | async-done | bytes 5767184 | tf_op jit(solution)/shard_map/all_gather | solution.py:157
  334.6 8.8 multiply_convert_fusion.1
  343.4 7.8 multiply_reduce_fusion
  356.4 102.9 %while.29 = (s32[]{:T(128)}, f32[256,16,64]{0,2,1:T(8,128)}, bf16[4,512,2048]{2,1,0:T(8,128)(2,1)}, s32[4]{0:T(128)S(1)}, bf16[2048,2048]{0,1:T(8,128)(2,1)}, /*...) while((s32[]{:T(128)}, f32[256,16,64]{0,2,1:T(8,128)}, ...), condition=%wide.region_11.12_spmd.clone, body=%wide.region_10.11_spmd.clone.sunk | while | flops 1369309184 | bytes 118946184 | solution.py:132
  369.4 5.2 fusion.131
  395.2 5.2 fusion.131
  421.0 5.2 fusion.131
  446.8 5.2 fusion.131
  462.8 5.6 convolution_convert_fusion.1
  469.6 8.1 convolution_convert_fusion
  481.2 127.3 %reduce-scatter.6.cloned.1.call-done = bf16[256,2048]{1,0:T(8,128)(2,1)} async-done(((bf16[2048,2048]{1,0:T(8,128)(2,1)}), bf16[256,2048]{1,0:T(8,128)(2,1)}) %reduce-scatter.6.cloned.1.call-update) | async-done | bytes 1048592 | tf_op jit(solution)/shard_map/reduce_scatter | solution.py:220
  608.5 5.8 convolution_convert_fusion.2
  614.4 27.8 %reduce-scatter.10.cloned.1.call-done = bf16[256,1024]{1,0:T(8,128)(2,1)} async-done(((bf16[1024,1024]{1,0:T(8,128)(2,1)}), bf16[256,1024]{1,0:T(8,128)(2,1)}) %reduce-scatter.10.cloned.1.call-update) | async-done | bytes 524304 | tf_op jit(solution)/shard_map/reduce_scatter | solution.py:244
  642.2 58.0 %reduce-scatter.14.cloned.1.call-done = bf16[704,1024]{1,0:T(8,128)(2,1)} async-done(((bf16[2816,1024]{1,0:T(8,128)(2,1)}), bf16[704,1024]{1,0:T(8,128)(2,1)}) %reduce-scatter.14.cloned.1.call-update) | async-done | bytes 1441808 | tf_op jit(solution)/shard_map/reduce_scatter | solution.py:253
  700.2 95.0 %reduce-scatter.12.cloned.1.call-done = bf16[256,5632]{1,0:T(8,128)(2,1)} async-done(((bf16[1024,5632]{1,0:T(8,128)(2,1)}), bf16[256,5632]{1,0:T(8,128)(2,1)}) %reduce-scatter.12.cloned.1.call-update) | async-done | bytes 2883600 | tf_op jit(solution)/shard_map/reduce_scatter | solution.py:250
  795.3 60.9 %reduce-scatter.8.cloned.1.call-done = bf16[256,3072]{1,0:T(8,128)(2,1)} async-done(((bf16[1024,3072]{1,0:T(8,128)(2,1)}), bf16[256,3072]{1,0:T(8,128)(2,1)}) %reduce-scatter.8.cloned.1.call-update) | async-done | bytes 1572880 | tf_op jit(solution)/shard_map/reduce_scatter | solution.py:241
  857.5 5.6 fusion.35
  863.1 5.0 fusion.42
  868.1 6.1 all-reduce.4
  874.3 22.2 %all-reduce.2 = (bf16[256]{0:T(256)(128)(2,1)S(1)}, bf16[256]{0:T(256)(128)(2,1)S(1)}) all-reduce(bf16[256]{0:T(256)(128)(2,1)S(1)} %dynamic-slice.1, bf16[256]{0:T(256)(128)(2,1)S(1)} %dynamic-slice.3), channel_id=1, replica_groups=mesh['ctx'=8,'fsdp'=4] {'ctx'}, use_global_device_ids=true, to_apply=%region_16.17 | all-reduce | flops 512 | bytes 2048 | tf_op jit(solution)/shard_map/psum | solution.py:258
  898.2 136.6 %all-reduce.7.cloned.1.call-done = (bf16[256,1024]{1,0:T(8,128)(2,1)}, bf16[256,5632]{1,0:T(8,128)(2,1)}, bf16[704,1024]{1,0:T(8,128)(2,1)}) async-done(((bf16[256,1024]{1,0:T(8,128)(2,1)}, bf16[256,5632]{1,0:T(8,128)(2,1)}, bf16[704,1024]{1,0:T(8,128)(2,1)}), (bf16[256,1024]{1,0:T(8,128)(2,1)}, bf16[256,5632]{1,0:T(8,128)(2,1)}, bf16[704,1024]{1,0:T(8,128)(2,1)})) %all-reduce.7.cloned.1.call-update) | async-done | bytes 4849680 | tf_op jit(solution)/shard_map/psum | solution.py:262
  1043.7 168.8 %all-gather.20.cloned.1.call-done = bf16[2048,3072]{1,0:T(8,128)(2,1)} async-done(((bf16[256,3072]{1,0:T(8,128)(2,1)}), bf16[2048,3072]{1,0:T(8,128)(2,1)}) %all-gather.20.cloned.1.call-update) | async-done | bytes 12582928 | tf_op jit(solution)/shard_map/all_gather | solution.py:259
  1212.5 7.3 reduce_sum.100
  (250 shorter events, 185.8 us)
Async XLA Ops:
  7.2 51.5 %all-gather.10.cloned.1.call-start = ((), (), s32[]{:S(2)}) async-start(), calls=%async_computation.5 | async-start | bytes 7864320 | tf_op jit(solution)/shard_map/all_gather | solution.py:153
  7.9 181.9 %all-gather.12.cloned.1.call-start = ((), (), s32[]{:S(2)}) async-start(), calls=%async_computation.6 | async-start | bytes 9437184 | tf_op jit(solution)/shard_map/all_gather | solution.py:179
  14.6 48.9 %copy-start.21 = (f32[4,1,256]{2,1,0:T(1,128)}, f32[4,1,256]{2,1,0:T(1,128)S(1)}, u32[]{:S(2)}) copy-start(f32[4,1,256]{2,1,0:T(1,128)S(1)} %convert_element_type.152) | copy-start | bytes 12292
  15.8 47.7 %copy-start.23 = (f32[256]{0:T(256)}, f32[256]{0:T(256)S(1)}, u32[]{:S(2)}) copy-start(f32[256]{0:T(256)S(1)} %add_rsqrt_fusion.1) | copy-start | bytes 3076
  64.7 212.5 %all-gather.14.cloned.1.call-start = ((), (), s32[]{:S(2)}) async-start(), calls=%async_computation.7 | async-start | bytes 2621440 | tf_op jit(solution)/shard_map/all_gather | solution.py:154
  65.4 224.3 %all-gather.16.cloned.1.call-start = ((), (), s32[]{:S(2)}) async-start(), calls=%async_computation.8 | async-start | bytes 14417920 | tf_op jit(solution)/shard_map/all_gather | solution.py:156
  66.0 268.6 %all-gather.18.cloned.1.call-start = ((), (), s32[]{:S(2)}) async-start(), calls=%async_computation.9 | async-start | bytes 7208960 | tf_op jit(solution)/shard_map/all_gather | solution.py:157
  66.6 541.9 %reduce-scatter.6.cloned.1.call-start = ((), (), s32[]{:S(2)}) async-start(), calls=%async_computation.10 | async-start | bytes 9437184 | tf_op jit(solution)/shard_map/reduce_scatter | solution.py:220
  202.1 75.1 %copy-start.8 = (bf16[256,1024]{1,0:T(8,128)(2,1)S(1)}, bf16[256,1024]{1,0:T(8,128)(2,1)}, u32[]{:S(2)}) copy-start(bf16[256,1024]{1,0:T(8,128)(2,1)} %param.14) | copy-start | bytes 1572868
  210.2 5.9 copy-start
  228.9 5.8 copy-start
  247.2 6.0 copy-start
  265.6 5.9 copy-start
  277.1 22.0 %copy-start.9 = (bf16[256,16,64]{0,2,1:T(8,128)(2,1)}, bf16[256,16,64]{0,2,1:T(8,128)(2,1)S(1)}, u32[]{:S(2)}) copy-start(bf16[256,16,64]{0,2,1:T(8,128)(2,1)S(1)} %fusion.45) | copy-start | bytes 1572868
  279.8 71.5 %copy-start.3 = (f32[256,1024]{1,0:T(8,128)}, f32[256,1024]{1,0:T(8,128)S(1)}, u32[]{:S(2)}) copy-start(f32[256,1024]{1,0:T(8,128)S(1)} %get-tuple-element.409) | copy-start | bytes 3145732
  289.7 44.9 %copy-start.15 = (bf16[256,1024]{1,0:T(8,128)(2,1)S(1)}, bf16[256,1024]{1,0:T(8,128)(2,1)}, u32[]{:S(2)}) copy-start(bf16[256,1024]{1,0:T(8,128)(2,1)} %param.15) | copy-start | bytes 1572868
  343.4 7.8 copy-start.18
  343.4 7.8 copy-start.19
  343.4 7.9 copy-start.16
  343.4 8.2 copy-start.7
  446.8 5.2 copy-start.1
  459.3 182.9 %reduce-scatter.10.cloned.1.call-start = ((), (), s32[]{:S(2)}) async-start(), calls=%async_computation.12 | async-start | bytes 2621440 | tf_op jit(solution)/shard_map/reduce_scatter | solution.py:244
  462.7 237.5 %reduce-scatter.14.cloned.1.call-start = ((), (), s32[]{:S(2)}) async-start(), calls=%async_computation.14 | async-start | bytes 7208960 | tf_op jit(solution)/shard_map/reduce_scatter | solution.py:253
  468.4 326.8 %reduce-scatter.12.cloned.1.call-start = ((), (), s32[]{:S(2)}) async-start(), calls=%async_computation.13 | async-start | bytes 14417920 | tf_op jit(solution)/shard_map/reduce_scatter | solution.py:250
  477.8 130.7 %copy-start.22 = (f32[4,1,256]{2,1,0:T(1,128)S(1)}, f32[4,1,256]{2,1,0:T(1,128)}, u32[]{:S(2)}) copy-start(f32[4,1,256]{2,1,0:T(1,128)} %copy-done.21) | copy-start | bytes 12292
  477.8 130.7 %copy-start.24 = (f32[256]{0:T(256)S(1)}, f32[256]{0:T(256)}, u32[]{:S(2)}) copy-start(f32[256]{0:T(256)} %copy-done.23) | copy-start | bytes 3076
  477.8 378.4 %reduce-scatter.8.cloned.1.call-start = ((), (), s32[]{:S(2)}) async-start(), calls=%async_computation.11 | async-start | bytes 7864320 | tf_op jit(solution)/shard_map/reduce_scatter | solution.py:241
  614.3 241.9 %copy-start.28 = (u32[32]{0:T(128)S(1)}, u32[32]{0:T(128)}, u32[]{:S(2)}) copy-start(u32[32]{0:T(128)} %constant.85) | copy-start | bytes 388
  614.4 420.4 %all-reduce.7.cloned.1.call-start = ((), (), s32[]{:S(2)}) async-start(), calls=%async_computation.16 | async-start | bytes 9699328 | tf_op jit(solution)/shard_map/psum | solution.py:262
  795.3 417.2 %all-gather.20.cloned.1.call-start = ((), (), s32[]{:S(2)}) async-start(), calls=%async_computation.15 | async-start | bytes 14155776 | tf_op jit(solution)/shard_map/all_gather | solution.py:259
  857.5 5.6 copy-start.20
  1034.8 5.6 copy-start.12
  (24 other events, 84.1 us)
Sparse Core Ops, SparseCore 0:
  9.6 49.0 all-gather.9
  64.8 124.9 all-gather.11
  191.3 20.7 all-gather.13
  213.5 76.1 all-gather.15
  291.1 43.3 all-gather.17
  459.5 148.9 reduce-scatter.5
  611.8 30.4 reduce-scatter.9
  645.3 54.8 reduce-scatter.13
  703.0 92.2 reduce-scatter.11
  797.8 58.3 reduce-scatter.7
  860.2 174.5 all-reduce.6
  1037.1 175.3 all-gather.19
